TPU v7x, 32 devices: a whole 2x2x4 slice. The times are simulated.
32 devices in a mesh: heads: 2 (over y), seq: 16 (over z, x, core).
Axes of the slice: x: 2, y: 2, z: 4, core: 2. Of those that a mesh axis runs over, the one named last changes fastest.
Arguments:
- signal: bfloat16 [2048, 1280], P('seq', 'heads'), may hold values from -6 to 6
- b_in: bfloat16 [2048, 128], P('seq'), may hold values from -1.75 to 1.75
- c_in: bfloat16 [2048, 128], P('seq'), may hold values from -1.75 to 1.75
- step: float32 [20, 2048], P('heads', 'seq'), may hold values from 0.008 to 0.03
- decay_log: float32 [20, 2048], P('heads', 'seq'), may hold values from -2.3 to 0
- level_weight: float32 [8, 20, 2048], P(None, 'heads', 'seq'), may hold values from 0.02 to 4
- skip: float32 [20], P('heads'), may hold values from 0.5 to 1.5
- grad_out: bfloat16 [2048, 1280], P('seq', 'heads'), may hold values from -6 to 6
- state_cotangent: float32 [20, 128, 64], P('heads'), may hold values from -12 to 12
Outputs:
- output: bfloat16 [2048, 1280], P('seq', 'heads')
- dx: bfloat16 [2048, 1280], P('seq', 'heads')
- db: bfloat16 [2048, 128], P('seq')
- dc: bfloat16 [2048, 128], P('seq')
All inputs are finite; a program needn't handle non-finite values.
Results may differ from a plain program's by a relative error of at most 0.001.
Values may be sent and summed in bfloat16 or wider, within the bound.
A program may use at most 64 MiB of HBM per device.

v0:
```python
import jax
import jax.numpy as jnp
from jax import lax
from jax.sharding import PartitionSpec as P

P_SIZE = 64


HIGH = lax.Precision.HIGHEST


def from_partner(shard, axis, bit):
    return lax.ppermute(shard, axis, [(i, i ^ 1 << bit) for i in range(lax.axis_size(axis))])


def decay_table(cum_h, lower):
    diff = cum_h[:, None] - cum_h[None, :]
    return jnp.where(lower, jnp.exp(jnp.where(lower, diff, 0.0)), 0.0)


def on_device(signal, b_in, c_in, step, decay_log, level_weight, skip, grad_out, state_cotangent):
    tokens = signal.shape[0]
    heads = step.shape[0]
    x_rows = signal.astype(jnp.float32).reshape(tokens, heads, P_SIZE)
    dy_rows = grad_out.astype(jnp.float32).reshape(tokens, heads, P_SIZE)
    x_heads = signal.reshape(tokens, heads, P_SIZE).transpose(1, 0, 2)
    output_grad_heads = grad_out.reshape(tokens, heads, P_SIZE).transpose(1, 0, 2)
    b_rows = b_in.astype(jnp.float32)
    c_rows = c_in.astype(jnp.float32)
    cum = jnp.cumsum(decay_log, axis=1)
    row_positions = lax.broadcasted_iota(jnp.int32, (tokens, tokens), 0)
    col_ids = lax.broadcasted_iota(jnp.int32, (tokens, tokens), 1)
    lower = row_positions >= col_ids
    scores = jnp.dot(c_in, b_in.T, preferred_element_type=jnp.float32)

    def forward_head(args):
        cum_h, x_h, step_h = args
        weight_h = decay_table(cum_h, lower)
        inputs_h = step_h[:, None] * x_h.astype(jnp.float32)
        y_h = jnp.dot(scores * weight_h, inputs_h, precision=HIGH)
        tail_h = jnp.exp(cum_h[-1] - cum_h)
        state_h = jnp.dot((tail_h[:, None] * b_rows).T, inputs_h, precision=HIGH)
        return (y_h, state_h)

    y_heads, state = lax.map(forward_head, (cum, x_heads, step))
    y_local = y_heads.transpose(1, 0, 2)
    depth = lax.axis_size("seq").bit_length() - 1
    index = lax.axis_index("seq")
    coef = level_weight[:depth] * jnp.exp(cum)[None]
    total = state
    decay_sum = cum[:, -1]
    offset = jnp.zeros((heads,), jnp.float32)
    levels = []
    records = []
    for bit in range(depth):
        far_total, far_decay = from_partner((total, decay_sum), "seq", bit)
        upper = index >> bit & 1 == 1
        level = jnp.where(upper, jnp.exp(offset)[:, None, None] * far_total, 0.0)
        levels.append(level)
        records.append((upper, decay_sum, far_decay, offset))
        total = jnp.where(
            upper,
            total + jnp.exp(decay_sum)[:, None, None] * far_total,
            far_total + jnp.exp(far_decay)[:, None, None] * total,
        )
        offset = jnp.where(upper, offset + far_decay, offset)
        decay_sum = decay_sum + far_decay
    stacked = jnp.stack(levels)
    y_levels = jnp.einsum("kht,tn,khnp->thp", coef, c_rows, stacked, precision=HIGH)
    y_out = (
        (y_local + y_levels + skip[None, :, None] * x_rows)
        .astype(jnp.bfloat16)
        .reshape(tokens, heads * P_SIZE)
    )
    grad_levels = jnp.einsum("kht,tn,thp->khnp", coef, c_rows, dy_rows, precision=HIGH)
    dc_levels = jnp.einsum("kht,thp,khnp->tn", coef, dy_rows, stacked, precision=HIGH)
    carry = jnp.where(index == 0, state_cotangent, jnp.float32(0.0))
    for bit in reversed(range(depth)):
        upper, own_decay, far_decay, offset_k = records[bit]
        send = jnp.where(
            upper,
            jnp.exp(own_decay)[:, None, None] * carry
            + jnp.exp(offset_k)[:, None, None] * grad_levels[bit],
            carry,
        )
        keep = jnp.where(upper, carry, jnp.exp(far_decay)[:, None, None] * carry)
        carry = keep + from_partner(send, "seq", bit)

    def backward_head(sums, args):
        score_grad, db_state = sums
        cum_h, x_h, dy_h, step_h, carry_h = args
        weight_h = decay_table(cum_h, lower)
        tail_h = jnp.exp(cum_h[-1] - cum_h)
        raw = jnp.dot(dy_h, x_h.T, preferred_element_type=jnp.float32)
        score_grad = score_grad + raw * step_h[None, :] * weight_h
        in_grad_h = jnp.dot((scores * weight_h).T, dy_h.astype(jnp.float32), precision=HIGH)
        in_grad_h = in_grad_h + tail_h[:, None] * jnp.dot(b_rows, carry_h, precision=HIGH)
        inputs_h = step_h[:, None] * x_h.astype(jnp.float32)
        db_state = db_state + tail_h[:, None] * jnp.dot(inputs_h, carry_h.T, precision=HIGH)
        return ((score_grad, db_state), in_grad_h)

    start = (
        jnp.zeros((tokens, tokens), jnp.float32),
        jnp.zeros((tokens, b_rows.shape[1]), jnp.float32),
    )
    (score_grad, db_state), in_heads = lax.scan(
        backward_head, start, (cum, x_heads, output_grad_heads, step, carry)
    )
    in_grad = in_heads.transpose(1, 0, 2)
    dc_part = jnp.dot(score_grad, b_rows, precision=HIGH) + dc_levels
    db_part = jnp.dot(score_grad.T, c_rows, precision=HIGH) + db_state
    dx_out = (
        (skip[None, :, None] * dy_rows + step.T[:, :, None] * in_grad)
        .astype(jnp.bfloat16)
        .reshape(tokens, heads * P_SIZE)
    )
    db_sum, dc_sum = lax.psum((db_part, dc_part), "heads")
    db_out = db_sum.astype(jnp.bfloat16)
    dc_out = dc_sum.astype(jnp.bfloat16)
    return (y_out, dx_out, db_out, dc_out)


def solution(mesh):
    return jax.shard_map(
        on_device,
        mesh=mesh,
        in_specs=(
            P("seq", "heads"),
            P("seq", None),
            P("seq", None),
            P("heads", "seq"),
            P("heads", "seq"),
            P(None, "heads", "seq"),
            P("heads"),
            P("seq", "heads"),
            P("heads", None, None),
        ),
        out_specs=(P("seq", "heads"), P("seq", "heads"), P("seq", None), P("seq", None)),
        check_vma=False,
    )
```

profile of v0, /device:TPU:0, one launch (start us, length us, event | category | flops | bytes accessed | tf_op | source)
XLA Modules:
  0.0 135.1 jit_solution(12877675999122390506)
XLA Ops:
  0.6 1.0 reduce_window_sum.11
  2.3 1.1 copy.25
  5.5 27.0 %while.30 = (s32[]{:T(128)}, f32[10,128,64]{1,2,0:T(8,128)S(1)}, f32[10,128,64]{1,2,0:T(8,128)S(1)}, f32[10,128]{1,0:T(8,128)S(1)}, f32[128,128]{1,0:T(8,128)S(1...) while((s32[]{:T(128)}, f32[10,128,64]{1,2,0:T(8,128)S(1)}, ...), condition=%wide.region_2.3_spmd.clone.clone, body=%wide.region_1.2_spmd.clone.clone.sunk | while | flops 25297024 | bytes 270969 | solution.py:45
  34.2 2.6 %collective-permute-start.3 = (f32[10]{0:T(128)S(1)}, f32[10]{0:T(128)S(1)}, u32[]{:S(2)}, u32[]{:S(2)}) collective-permute-start(f32[10]{0:T(128)S(1)} %get-tuple-element.328), channel_id=1, source_target_pairs={{0,2},{1,3},{2,0},{3,1},{4,6},{5,7},{6,4},{7,5},{8,10},{9,11},{10,... | collective-permute-start | bytes 128 | tf_op jit(solution)/shard_map/ppermute | solution.py:13
  36.8 1.5 %collective-permute-done.3 = f32[10]{0:T(128)S(1)} collective-permute-done((f32[10]{0:T(128)S(1)}, f32[10]{0:T(128)S(1)}, u32[]{:S(2)}, u32[]{:S(2)}) %collective-permute-start.3) | collective-permute-done | bytes 72 | tf_op jit(solution)/shard_map/ppermute | solution.py:13
  38.4 2.2 %collective-permute-start.5 = (f32[10]{0:T(128)S(1)}, f32[10]{0:T(128)S(1)}, u32[]{:S(2)}, u32[]{:S(2)}) collective-permute-start(f32[10]{0:T(128)S(1)} %get-tuple-element.342), channel_id=1, source_target_pairs={{0,4},{1,5},{2,6},{3,7},{4,0},{5,1},{6,2},{7,3},{8,12},{9,13},{10,... | collective-permute-start | bytes 128 | tf_op jit(solution)/shard_map/ppermute | solution.py:13
  41.3 1.5 %collective-permute-start.2 = (f32[10,128,64]{1,2,0:T(8,128)S(1)}, f32[10,128,64]{1,2,0:T(8,128)S(1)}, u32[]{:S(2)}, u32[]{:S(2)}) collective-permute-start(f32[10,128,64]{1,2,0:T(8,128)S(1)} %get-tuple-element.330), channel_id=1, source_target_pairs={{0,2},{1,3},{2,0},{3,1},{4,6},{5,7},{6,4},{7,5},{8,10},{9,11},{10,... | collective-permute-start | bytes 983048 | tf_op jit(solution)/shard_map/ppermute | solution.py:13
  42.9 2.7 %collective-permute-start.8 = (f32[10,128,64]{1,2,0:T(8,128)S(1)}, f32[10,128,64]{1,2,0:T(8,128)S(1)}, u32[]{:S(2)}, u32[]{:S(2)}) collective-permute-start(f32[10,128,64]{1,2,0:T(8,128)S(1)} %fusion.100), channel_id=1, source_target_pairs={{0,8},{1,9},{2,10},{3,11},{4,12},{5,13},{6,14},{7,15},{8,0},{9,1},... | collective-permute-start | bytes 983048 | tf_op jit(solution)/shard_map/ppermute | solution.py:13
  45.6 4.4 %collective-permute-done.2 = f32[10,128,64]{1,2,0:T(8,128)S(1)} collective-permute-done((f32[10,128,64]{1,2,0:T(8,128)S(1)}, f32[10,128,64]{1,2,0:T(8,128)S(1)}, u32[]{:S(2)}, u32[]{:S(2)}) %collective-permute-start.2) | collective-permute-done | bytes 327712 | tf_op jit(solution)/shard_map/ppermute | solution.py:13
  50.5 2.7 %collective-permute-start.7 = (f32[10]{0:T(128)S(1)}, f32[10]{0:T(128)S(1)}, u32[]{:S(2)}, u32[]{:S(2)}) collective-permute-start(f32[10]{0:T(128)S(1)} %get-tuple-element.322), channel_id=1, source_target_pairs={{0,8},{1,9},{2,10},{3,11},{4,12},{5,13},{6,14},{7,15},{8,0},{9,1},... | collective-permute-start | bytes 128 | tf_op jit(solution)/shard_map/ppermute | solution.py:13
  53.2 6.3 %collective-permute-done.7 = f32[10]{0:T(128)S(1)} collective-permute-done((f32[10]{0:T(128)S(1)}, f32[10]{0:T(128)S(1)}, u32[]{:S(2)}, u32[]{:S(2)}) %collective-permute-start.7) | collective-permute-done | bytes 72 | tf_op jit(solution)/shard_map/ppermute | solution.py:13
  59.5 5.3 %collective-permute-done.4 = f32[10,128,64]{1,2,0:T(8,128)S(1)} collective-permute-done((f32[10,128,64]{1,2,0:T(8,128)S(1)}, f32[10,128,64]{1,2,0:T(8,128)S(1)}, u32[]{:S(2)}, u32[]{:S(2)}) %collective-permute-start.4) | collective-permute-done | bytes 327712 | tf_op jit(solution)/shard_map/ppermute | solution.py:13
  64.8 1.1 select_bitcast_fusion.1
  65.9 2.4 %collective-permute-start.6 = (f32[10,128,64]{1,2,0:T(8,128)}, f32[10,128,64]{1,2,0:T(8,128)}, u32[]{:S(2)}, u32[]{:S(2)}) collective-permute-start(f32[10,128,64]{1,2,0:T(8,128)} %get-tuple-element.334), channel_id=1, source_target_pairs={{0,8},{1,9},{2,10},{3,11},{4,12},{5,13},{6,14},{7,15},{8,0},{9,1},... | collective-permute-start | bytes 983048 | tf_op jit(solution)/shard_map/ppermute | solution.py:13
  68.3 11.8 %collective-permute-done.9 = f32[10,128,64]{1,2,0:T(8,128)S(1)} collective-permute-done((f32[10,128,64]{1,2,0:T(8,128)S(1)}, f32[10,128,64]{1,2,0:T(8,128)S(1)}, u32[]{:S(2)}, u32[]{:S(2)}) %collective-permute-start.9) | collective-permute-done | bytes 327712 | tf_op jit(solution)/shard_map/ppermute | solution.py:13
  80.2 0.9 fusion.94
  81.1 1.0 collective-permute-start.10
  82.2 1.1 select_bitcast_fusion
  83.4 6.6 %collective-permute-done.10 = f32[10,128,64]{1,2,0:T(8,128)S(1)} collective-permute-done((f32[10,128,64]{1,2,0:T(8,128)}, f32[10,128,64]{1,2,0:T(8,128)S(1)}, u32[]{:S(2)}, u32[]{:S(2)}) %collective-permute-start.10) | collective-permute-done | bytes 327712 | tf_op jit(solution)/shard_map/ppermute | solution.py:13
  89.9 1.6 %fusion.91 = f32[10,128,64]{1,2,0:T(8,128)} fusion(f32[4,10,128,64]{2,3,1,0:T(8,128)S(1)} %convolution_bitcast_fusion.2, f32[10]{0:T(128)} %copy-done.19, pred[]{:T(512)S(6)} %eq.15, f32[10,128,64]{1,2,0:T(8,128)S(1)} %collective-permute-done.10, f32[10,128,64]{1,2,0:T(8,128)S(1)} %get-tuple-element.320, f32[10]{0:T(128)} %copy-done.14, pred[]{:T(512)S(6)} %eq.16), kind=kLoop, calls=%fused_computation.101 | loop fusion | flops 491520 | bytes 1310802 | tf_op jit(solution)/shard_map/jit(_where)/select_n | solution.py:80
  91.6 3.5 %fusion.83 = bf16[128,10,64]{0,2,1:T(8,128)(2,1)S(1)} fusion(f32[10,128,64]{1,2,0:T(8,128)S(1)} %copy-done.6, f32[128,128]{1,0:T(8,128)S(1)} %convert.7, f32[128,4,10]{0,1,2:T(4,128)S(1)} %get-tuple-element.336, f32[1,10,128,64]{2,3,0,1:T(8,128)S(1)} %select_bitcast_fusion, f32[1,10,128,64]{2,3,0,1:T(8,128)S(1)} %copy-done.2, ...), kind=kOutput, calls=%fused_computation.87 | convolution fusion | flops 505364480 | bytes 2052136 | tf_op jit(solution)/shard_map/kht,tn,khnp->thp/dot_general | solution.py:69
  95.9 3.2 %convolution_bitcast_fusion.3 = f32[128,128]{1,0:T(8,128)S(1)} fusion(f32[1,10,128,64]{2,3,0,1:T(8,128)} %copy-done.4, f32[1,10,128,64]{2,3,0,1:T(8,128)S(1)} %copy-done.3, f32[1,10,128,64]{2,3,0,1:T(8,128)S(1)} %get-tuple-element.331, f32[1,10,128,64]{2,3,0,1:T(8,128)S(1)} %copy-done.8, f32[128,10,64]{0,2,1:T(8,128)S(1)} %reshape.85, ...), kind=kOutput, calls=%fused_computation.90 | convolution fusion | flops 504627200 | bytes 1724416 | tf_op jit(solution)/shard_map/kht,thp,khnp->tn/dot_general | solution.py:76
  99.9 23.3 %while.31 = (s32[]{:T(128)}, f32[128,128]{1,0:T(8,128)S(1)}, f32[128,128]{1,0:T(8,128)S(1)}, f32[10,128,64]{1,2,0:T(8,128)S(1)}, bf16[10,128,64]{1,2,0:T(8,128)(...) while((s32[]{:T(128)}, f32[128,128]{1,0:T(8,128)S(1)}, ...), condition=%wide.region_4.5_spmd.clone.clone, body=%wide.region_3.4_spmd.clone.clone.sunk | while | flops 40140928 | bytes 666792 | solution.py:106
  124.6 10.5 %all-reduce.2 = (bf16[128,128]{1,0:T(8,128)(2,1)}, bf16[128,128]{1,0:T(8,128)(2,1)}) all-reduce(f32[128,128]{1,0:T(8,128)S(1)} %convolution_add_fusion.1, f32[128,128]{1,0:T(8,128)S(1)} %convolution_add_fusion), channel_id=1, replica_groups=mesh['heads'=2,'seq'=16] {'heads'}, use_global_device_ids=true, to_apply=%region_5.6 | all-reduce | flops 32768 | bytes 196608 | tf_op jit(solution)/shard_map/psum | solution.py:117
  (245 shorter events, 57.9 us)
Async XLA Ops:
  1.8 32.4 %collective-permute-start.1 = (f32[10]{0:T(128)S(1)}, f32[10]{0:T(128)S(1)}, u32[]{:S(2)}, u32[]{:S(2)}) collective-permute-start(f32[10]{0:T(128)S(1)} %slice_reduce_fusion), channel_id=1, source_target_pairs={{0,1},{1,0},{2,3},{3,2},{4,5},{5,4},{6,7},{7,6},{8,9},{9,8},{10,11... | collective-permute-start | bytes 128 | tf_op jit(solution)/shard_map/ppermute | solution.py:13
  5.4 27.8 %copy-start.10 = (bf16[128,640]{1,0:T(8,128)(2,1)S(1)}, bf16[128,640]{1,0:T(8,128)(2,1)}, u32[]{:S(2)}) copy-start(bf16[128,640]{1,0:T(8,128)(2,1)} %param.20) | copy-start | bytes 491524
  5.4 27.9 %copy-start.13 = (f32[8,10,128]{2,0,1:T(8,128)S(1)}, f32[8,10,128]{2,0,1:T(8,128)}, u32[]{:S(2)}) copy-start(f32[8,10,128]{2,0,1:T(8,128)} %param.18) | copy-start | bytes 122884
  5.4 28.0 %copy-start.1 = (bf16[128,128]{1,0:T(8,128)(2,1)S(1)}, bf16[128,128]{1,0:T(8,128)(2,1)}, u32[]{:S(2)}) copy-start(bf16[128,128]{1,0:T(8,128)(2,1)} %param.15) | copy-start | bytes 98308
  32.5 8.1 %collective-permute-start = (f32[10,128,64]{1,2,0:T(8,128)S(1)}, f32[10,128,64]{1,2,0:T(8,128)S(1)}, u32[]{:S(2)}, u32[]{:S(2)}) collective-permute-start(f32[10,128,64]{1,2,0:T(8,128)S(1)} %get-tuple-element.123), channel_id=1, source_target_pairs={{0,1},{1,0},{2,3},{3,2},{4,5},{5,4},{6,7},{7,6},{8,9},{9,8},{10,11... | collective-permute-start | bytes 983048 | tf_op jit(solution)/shard_map/ppermute | solution.py:13
  33.4 9.4 %copy-start = (f32[10,128,64]{1,2,0:T(8,128)S(1)}, f32[10,128,64]{1,2,0:T(8,128)}, u32[]{:S(2)}) copy-start(f32[10,128,64]{1,2,0:T(8,128)} %param.21) | copy-start | bytes 983044
  34.2 46.9 %copy-start.19 = (f32[10]{0:T(128)}, f32[10]{0:T(128)S(1)}, u32[]{:S(2)}) copy-start(f32[10]{0:T(128)S(1)} %get-tuple-element.345) | copy-start | bytes 124
  34.2 4.1 %collective-permute-start.3 = (f32[10]{0:T(128)S(1)}, f32[10]{0:T(128)S(1)}, u32[]{:S(2)}, u32[]{:S(2)}) collective-permute-start(f32[10]{0:T(128)S(1)} %get-tuple-element.328), channel_id=1, source_target_pairs={{0,2},{1,3},{2,0},{3,1},{4,6},{5,7},{6,4},{7,5},{8,10},{9,11},{10,... | collective-permute-start | bytes 128 | tf_op jit(solution)/shard_map/ppermute | solution.py:13
  38.3 11.8 %copy-start.17 = (f32[10]{0:T(128)}, f32[10]{0:T(128)S(1)}, u32[]{:S(2)}) copy-start(f32[10]{0:T(128)S(1)} %get-tuple-element.344) | copy-start | bytes 124
  38.3 42.8 %copy-start.14 = (f32[10]{0:T(128)}, f32[10]{0:T(128)S(1)}, u32[]{:S(2)}) copy-start(f32[10]{0:T(128)S(1)} %get-tuple-element.343) | copy-start | bytes 124
  38.4 4.4 %collective-permute-start.5 = (f32[10]{0:T(128)S(1)}, f32[10]{0:T(128)S(1)}, u32[]{:S(2)}, u32[]{:S(2)}) collective-permute-start(f32[10]{0:T(128)S(1)} %get-tuple-element.342), channel_id=1, source_target_pairs={{0,4},{1,5},{2,6},{3,7},{4,0},{5,1},{6,2},{7,3},{8,12},{9,13},{10,... | collective-permute-start | bytes 128 | tf_op jit(solution)/shard_map/ppermute | solution.py:13
  41.3 8.7 %collective-permute-start.2 = (f32[10,128,64]{1,2,0:T(8,128)S(1)}, f32[10,128,64]{1,2,0:T(8,128)S(1)}, u32[]{:S(2)}, u32[]{:S(2)}) collective-permute-start(f32[10,128,64]{1,2,0:T(8,128)S(1)} %get-tuple-element.330), channel_id=1, source_target_pairs={{0,2},{1,3},{2,0},{3,1},{4,6},{5,7},{6,4},{7,5},{8,10},{9,11},{10,... | collective-permute-start | bytes 983048 | tf_op jit(solution)/shard_map/ppermute | solution.py:13
  42.8 39.3 %copy-start.20 = (f32[10]{0:T(128)}, f32[10]{0:T(128)S(1)}, u32[]{:S(2)}) copy-start(f32[10]{0:T(128)S(1)} %get-tuple-element.339) | copy-start | bytes 124
  42.9 16.6 %collective-permute-start.8 = (f32[10,128,64]{1,2,0:T(8,128)S(1)}, f32[10,128,64]{1,2,0:T(8,128)S(1)}, u32[]{:S(2)}, u32[]{:S(2)}) collective-permute-start(f32[10,128,64]{1,2,0:T(8,128)S(1)} %fusion.100), channel_id=1, source_target_pairs={{0,8},{1,9},{2,10},{3,11},{4,12},{5,13},{6,14},{7,15},{8,0},{9,1},... | collective-permute-start | bytes 983048 | tf_op jit(solution)/shard_map/ppermute | solution.py:13
  50.1 14.7 %collective-permute-start.4 = (f32[10,128,64]{1,2,0:T(8,128)S(1)}, f32[10,128,64]{1,2,0:T(8,128)S(1)}, u32[]{:S(2)}, u32[]{:S(2)}) collective-permute-start(f32[10,128,64]{1,2,0:T(8,128)S(1)} %get-tuple-element.332), channel_id=1, source_target_pairs={{0,4},{1,5},{2,6},{3,7},{4,0},{5,1},{6,2},{7,3},{8,12},{9,13},{10,... | collective-permute-start | bytes 983048 | tf_op jit(solution)/shard_map/ppermute | solution.py:13
  50.5 9.0 %collective-permute-start.7 = (f32[10]{0:T(128)S(1)}, f32[10]{0:T(128)S(1)}, u32[]{:S(2)}, u32[]{:S(2)}) collective-permute-start(f32[10]{0:T(128)S(1)} %get-tuple-element.322), channel_id=1, source_target_pairs={{0,8},{1,9},{2,10},{3,11},{4,12},{5,13},{6,14},{7,15},{8,0},{9,1},... | collective-permute-start | bytes 128 | tf_op jit(solution)/shard_map/ppermute | solution.py:13
  65.9 14.3 %collective-permute-start.9 = (f32[10,128,64]{1,2,0:T(8,128)S(1)}, f32[10,128,64]{1,2,0:T(8,128)S(1)}, u32[]{:S(2)}, u32[]{:S(2)}) collective-permute-start(f32[10,128,64]{1,2,0:T(8,128)S(1)} %get-tuple-element.337), channel_id=1, source_target_pairs={{0,4},{1,5},{2,6},{3,7},{4,0},{5,1},{6,2},{7,3},{8,12},{9,13},{10,... | collective-permute-start | bytes 983048 | tf_op jit(solution)/shard_map/ppermute | solution.py:13
  65.9 16.4 %collective-permute-start.6 = (f32[10,128,64]{1,2,0:T(8,128)}, f32[10,128,64]{1,2,0:T(8,128)}, u32[]{:S(2)}, u32[]{:S(2)}) collective-permute-start(f32[10,128,64]{1,2,0:T(8,128)} %get-tuple-element.334), channel_id=1, source_target_pairs={{0,8},{1,9},{2,10},{3,11},{4,12},{5,13},{6,14},{7,15},{8,0},{9,1},... | collective-permute-start | bytes 983048 | tf_op jit(solution)/shard_map/ppermute | solution.py:13
  81.1 8.8 %collective-permute-start.10 = (f32[10,128,64]{1,2,0:T(8,128)}, f32[10,128,64]{1,2,0:T(8,128)S(1)}, u32[]{:S(2)}, u32[]{:S(2)}) collective-permute-start(f32[10,128,64]{1,2,0:T(8,128)} %get-tuple-element.319), channel_id=1, source_target_pairs={{0,2},{1,3},{2,0},{3,1},{4,6},{5,7},{6,4},{7,5},{8,10},{9,11},{10,... | collective-permute-start | bytes 983048 | tf_op jit(solution)/shard_map/ppermute | solution.py:13
  82.1 9.4 %copy-start.7 = (f32[1,10,128,64]{2,3,0,1:T(8,128)S(1)}, f32[1,10,128,64]{2,3,0,1:T(8,128)}, u32[]{:S(2)}) copy-start(f32[1,10,128,64]{2,3,0,1:T(8,128)} %get-tuple-element.329) | copy-start | bytes 983044
  83.4 11.7 %copy-start.4 = (f32[1,10,128,64]{2,3,0,1:T(8,128)}, f32[1,10,128,64]{2,3,0,1:T(8,128)S(1)}, u32[]{:S(2)}) copy-start(f32[1,10,128,64]{2,3,0,1:T(8,128)S(1)} %select_bitcast_fusion) | copy-start | bytes 983044
  91.5 7.6 %collective-permute-start.11 = (f32[10,128,64]{1,2,0:T(8,128)}, f32[10,128,64]{1,2,0:T(8,128)S(1)}, u32[]{:S(2)}, u32[]{:S(2)}) collective-permute-start(f32[10,128,64]{1,2,0:T(8,128)} %fusion.91), channel_id=1, source_target_pairs={{0,1},{1,0},{2,3},{3,2},{4,5},{5,4},{6,7},{7,6},{8,9},{9,8},{10,11... | collective-permute-start | bytes 983048 | tf_op jit(solution)/shard_map/ppermute | solution.py:13
  99.9 23.3 %copy-start.9 = (bf16[128,128]{1,0:T(8,128)(2,1)S(1)}, bf16[128,128]{1,0:T(8,128)(2,1)}, u32[]{:S(2)}) copy-start(bf16[128,128]{1,0:T(8,128)(2,1)} %param.14) | copy-start | bytes 98308
  99.9 23.7 %copy-start.22 = (f32[10]{0:T(128)S(1)}, f32[10]{0:T(128)}, u32[]{:S(2)}) copy-start(f32[10]{0:T(128)} %param.19) | copy-start | bytes 124
  (11 other events, 47.5 us)
where the time goes:
time: 136 us; the launch traced here: 135 us
  waiting for transfers between devices  36 us (26%)
  matrix products  25.4 us (19%)
  local copies, waits for them, and re-layouts  23.9 us (18%)
  other arithmetic  20.9 us (15%)
  starting transfers between devices  16.1 us (12%)
  blocking collectives  10.5 us (8%)
    ppermute x12, waiting for transfers between devices, from_partner(): lax.ppermute(shard, axis, [(i, i ^ 1 << bit) for i in range(lax.axis_size...  36 us
    ppermute x12, starting transfers between devices, from_partner(): lax.ppermute(shard, axis, [(i, i ^ 1 << bit) for i in range(lax.axis_size...  16.1 us
    psum x1, blocking collectives, on_device(): db_sum, dc_sum = lax.psum((db_part, dc_part), 'heads')  10.5 us
    mul x10, local copies, waits for them, and re-layouts, forward_head(): inputs_h = step_h[:, None] * x_h.astype(jnp.float32)  6.98 us
    exp x10, other arithmetic, forward_head(): tail_h = jnp.exp(cum_h[-1] - cum_h)  6.56 us
    exp x10, other arithmetic, backward_head(): tail_h = jnp.exp(cum_h[-1] - cum_h)  6.56 us
    slice x10, local copies, waits for them, and re-layouts, forward_head(): tail_h = jnp.exp(cum_h[-1] - cum_h)  5.82 us
    slice x10, local copies, waits for them, and re-layouts, backward_head(): tail_h = jnp.exp(cum_h[-1] - cum_h)  5.82 us
  transfers between devices with their start and end apart: 12, of which 7 were waited for; matrix products, arithmetic and copies ran while one was open for 30% of the time, Pallas kernels for 0%

commit v1 on v0

v1 whole, which is shorter than its diff:
```python
import functools

import jax
import jax.numpy as jnp
from jax import lax
from jax.experimental import pallas as pl
from jax.experimental.pallas import tpu as pltpu
from jax.sharding import PartitionSpec as P

MESH = pl.DeviceIdType.MESH
HIGH = lax.Precision.HIGHEST
F32 = jnp.float32
BF16 = jnp.bfloat16


def split(v):
    hi = v.astype(BF16)
    return hi, (v - hi.astype(F32)).astype(BF16)


def dot(a, b, ca, cb):
    return lax.dot_general(a, b, (((ca,), (cb,)), ((), ())), preferred_element_type=F32)


def kernel(
    n, depth, nh, heads, width, has_rest,
    x_ref, b_ref, c_ref, step_ref, decay_ref, lw_ref, skip_ref, dy_ref, cot_ref,
    y_out, dx_out, db_out, dc_out,
    gall, s_buf, t1, f, tq, g, rc, gh, rx, g1, r0, cs, cr, dt,
    v_hi, v_lo, coefx, u_hi, u_lo, tsx, y_acc, dx_acc, sg, dcl, hx,
    ssem, rsem, gs_sem, gr_sem, hs_sem, hr_sem,
):
    me = lax.axis_index("seq")
    mh = lax.axis_index("heads")
    tokens = x_ref.shape[0]
    rows = b_ref.shape[1]
    half, quarter = rows // 2, rows // 4
    psize = width // heads
    core = me % 2
    xbit = (me // 2) % 2
    half_own = pl.multiple_of(core * half, half)
    half_other = pl.multiple_of((1 - core) * half, half)
    q_own = pl.multiple_of(core * half + xbit * quarter, quarter)

    def bit(k):
        return (me // (1 << k)) % 2

    def partner(k):
        return me + (1 << k) * (1 - 2 * bit(k))

    barrier = pltpu.get_barrier_semaphore()

    def greet(j, carry):
        pl.semaphore_signal(barrier, inc=1, device_id={"seq": (me + j) % n}, device_id_type=MESH)
        return carry

    lax.fori_loop(1, n, greet, 0)
    for j in range(1, nh):
        pl.semaphore_signal(barrier, inc=1, device_id={"heads": (mh + j) % nh}, device_id_type=MESH)

    pending = []

    def copy(idx, src, dst, k):
        return pltpu.make_async_remote_copy(
            src_ref=src, dst_ref=dst, send_sem=ssem.at[idx], recv_sem=rsem.at[idx],
            device_id={"seq": partner(k)}, device_id_type=MESH,
        )

    names = {}

    def send(name, src, dst, k, when=None):
        idx = names.setdefault(name, len(names))
        cp = copy(idx, src, dst, k)
        pending.append((cp, when))
        if when is None:
            cp.start()
        else:
            pl.when(when)(cp.start)

    def recv(name, dst, k, when=None):
        idx = names[name]
        cp = copy(idx, dst, dst, k)
        if when is None:
            cp.wait_recv()
        else:
            pl.when(when)(cp.wait_recv)

    hpad = -(-heads // 16) * 16
    hrow = lax.broadcasted_iota(jnp.int32, (hpad, width), 0)
    hcol = lax.broadcasted_iota(jnp.int32, (hpad, width), 1)
    e1 = jnp.where((hcol >= hrow * psize) & (hcol < (hrow + 1) * psize), 1.0, 0.0).astype(BF16)
    e3 = jnp.concatenate([e1, e1, e1], axis=0)

    def pad(v):
        return jnp.concatenate([v, jnp.zeros((hpad - heads, v.shape[1]), F32)], axis=0)

    def expand(v):
        p0 = v.astype(BF16)
        rest = v - p0.astype(F32)
        p1 = rest.astype(BF16)
        p2 = (rest - p1.astype(F32)).astype(BF16)
        return dot(jnp.concatenate([p0, p1, p2], axis=0), e3, 0, 0)

    ti = lax.broadcasted_iota(jnp.int32, (tokens, tokens), 0)
    tj = lax.broadcasted_iota(jnp.int32, (tokens, tokens), 1)
    lower = ti >= tj
    step = pad(step_ref[...])
    cum = jnp.dot(pad(decay_ref[...]), jnp.where(ti <= tj, 1.0, 0.0), precision=HIGH,
                  preferred_element_type=F32)
    gall[me] = expand(cum)[tokens - 1:tokens, :]

    x = x_ref[...]
    dy = dy_ref[...]
    b = b_ref[...]
    c = c_ref[...]

    pl.semaphore_wait(barrier, n - 1 + nh - 1)

    def share(j, carry):
        pltpu.make_async_remote_copy(
            src_ref=gall.at[me], dst_ref=gall.at[me], send_sem=gs_sem, recv_sem=gr_sem,
            device_id={"seq": (me + j) % n}, device_id_type=MESH,
        ).start()
        return carry

    lax.fori_loop(1, n, share, 0)

    tail = jnp.exp(cum[:, tokens - 1:tokens] - cum)
    ts = expand(tail * step)
    tsx[...] = ts
    uh, ul = split(ts * x.astype(F32))
    u_hi[...] = uh
    u_lo[...] = ul
    s_buf[...] = dot(b, uh, 0, 0) + dot(b, ul, 0, 0)
    send("F0", s_buf, f.at[0], 0)

    ecum = jnp.exp(cum)
    for k in range(depth):
        @pl.when(bit(k) == 1)
        def _():
            coef = expand(pad(lw_ref[k]) * ecum)
            coefx[k] = coef
            vh, vl = split(coef * dy.astype(F32))
            v_hi[k] = vh
            v_lo[k] = vl
            g[k] = dot(c, vh, 0, 0) + dot(c, vl, 0, 0)
        if k == 0:
            send("R0", g.at[0], r0, 0, bit(0) == 1)

    everything = pltpu.make_async_copy(gall.at[pl.ds(0, n - 1)], gall.at[pl.ds(0, n - 1)], gr_sem)
    everything.wait()
    windows = lax.broadcasted_iota(jnp.int32, (n, 1, width), 0)
    gv = gall[...]

    def retention(mask):
        return jnp.exp(jnp.sum(jnp.where(mask, gv, 0.0), axis=0))

    up = [retention((windows >> k) == ((me >> k) | 1)) for k in range(depth)]
    off = [None] + [retention(((windows >> k) == (me >> k)) & (windows < me)) for k in range(1, depth)]
    after = retention(windows > me)

    order = [1] + list(range(depth - 1, 1, -1))
    for k in order:
        @pl.when(bit(k) == 1)
        def _():
            g[k] = g[k] * off[k]
        send(("RC", k), g.at[k, pl.ds(half_other, half)], rc.at[k], 0, bit(k) == 1)

    def merge(k, own, far):
        is_up = bit(k) == 1
        return jnp.where(is_up, own + up[k] * far, far + up[k] * own)

    recv("F0", f.at[0], 0)
    own_rows = pl.ds(half_own, half)
    t1[...] = merge(0, s_buf[own_rows], f[0, own_rows])
    send("F1", t1, f.at[1, own_rows], 1)

    scores = dot(c, b, 1, 1)
    cum_t = cum.T
    left = lax.broadcasted_iota(jnp.int32, (tokens, 2 * psize), 1) < psize
    zero = jnp.zeros((tokens, 2 * psize), BF16)
    sg[...] = jnp.zeros_like(sg)

    def pair(p):
        lanes = slice(p * 2 * psize, (p + 1) * 2 * psize)
        xp, dyp = x[:, lanes], dy[:, lanes]
        xs = [jnp.where(left, xp, zero), jnp.where(left, zero, xp)]
        dys = [jnp.where(left, dyp, zero), jnp.where(left, zero, dyp)]
        his, los = [], []
        total = None
        for a in range(2):
            h = 2 * p + a
            diff = cum_t[:, h:h + 1] - cum[h:h + 1, :]
            w = jnp.where(lower, jnp.exp(jnp.where(lower, diff, 0.0)), 0.0) * step[h:h + 1, :]
            part = dot(dys[a], xs[a], 1, 1) * w
            total = part if total is None else total + part
            hi, lo = split(scores * w)
            his.append(hi)
            los.append(lo)
        sg[...] += total
        xcat = jnp.concatenate(xs, axis=0)
        dycat = jnp.concatenate(dys, axis=0)
        gain = jnp.where(left[:1], skip_ref[2 * p], skip_ref[2 * p + 1])
        y_acc[:, lanes] = (
            dot(jnp.concatenate(his, axis=1), xcat, 1, 0) + dot(jnp.concatenate(los, axis=1), xcat, 1, 0)
            + gain * xp.astype(F32))
        dx_acc[:, lanes] = (
            dot(jnp.concatenate(his, axis=0), dycat, 0, 0) + dot(jnp.concatenate(los, axis=0), dycat, 0, 0)
            + gain * dyp.astype(F32))

    pairs = list(range(heads // 2))

    def some(count):
        for _ in range(count):
            if pairs:
                pair(pairs.pop(0))

    some(1)
    for k in order:
        recv(("RC", k), rc.at[k], 0, bit(k) == 1)

        @pl.when(bit(k) == 1)
        def _():
            gh[k] = g[k, own_rows] + rc[k]
        if k >= 2:
            send(("RX", k), gh.at[k, pl.ds(pl.multiple_of((1 - xbit) * quarter, quarter), quarter)],
                 rx.at[k], 1, bit(k) == 1)
        else:
            send("R1X", gh.at[1], g1.at[own_rows], 1, bit(1) == 1)

    own_q = pl.ds(q_own, quarter)
    q_in_half = pl.ds(pl.multiple_of(xbit * quarter, quarter), quarter)
    recv("F1", f.at[1, own_rows], 1)
    tq[2] = merge(1, t1[q_in_half], f[1, own_q])
    top = depth - 1
    send(("F", 2), tq.at[2], f.at[2, own_q], 2, bit(2) == 0 if top == 2 else None)
    send("F1C", f.at[1, own_rows], f.at[1, own_rows], 0, bit(1) == 1)
    some(1)

    recv("R1X", g1.at[own_rows], 1, bit(1) == 0)
    send("R1A", g1.at[own_rows], g1.at[own_rows], 0, bit(1) == 0)
    cs[0] = jnp.zeros((quarter, width), F32)
    carry_slot = cs.at[0]

    def slab_grad(k):
        recv(("RX", k), rx.at[k], 1, bit(k) == 1)

    def level_full(k):
        recv(("FX", k), f.at[k, pl.ds(pl.multiple_of(core * half + (1 - xbit) * quarter, quarter), quarter)], 1,
             bit(k) == 1)
        send(("FC", k), f.at[k, own_rows], f.at[k, own_rows], 0, bit(k) == 1)

    carry = None
    for r in range(2, depth):
        kb = top - (r - 2)
        slab_grad(kb)
        is_up = bit(kb) == 1
        grad = jnp.where(is_up, gh[kb, q_in_half] + rx[kb], 0.0)
        if carry is None:
            cs[kb] = grad
            send(("C", kb), cs.at[kb], cr.at[kb], kb, is_up)
        else:
            cs[kb] = jnp.where(is_up, up[kb] * carry + grad, carry)
            send(("C", kb), cs.at[kb], cr.at[kb], kb)
        some(1)
        recv(("F", r), f.at[r, own_q], r, bit(r) == 1 if r == top else None)
        if r < top:
            tq[r + 1] = merge(r, tq[r], f[r, own_q])
            send(("F", r + 1), tq.at[r + 1], f.at[r + 1, own_q], r + 1, bit(r + 1) == 0 if r + 1 == top else None)
        send(("FX", r), f.at[r, own_q], f.at[r, own_q], 1, bit(r) == 1)
        if r > 2:
            level_full(r - 1)
        recv(("C", kb), cr.at[kb], kb, bit(kb) == 0 if kb == top else None)
        if carry is None:
            carry = jnp.where(is_up, 0.0, cr[kb])
        else:
            carry = jnp.where(is_up, carry, up[kb] * carry) + cr[kb]
    dt[own_q] = carry
    send("CX", dt.at[own_q], dt.at[own_q], 1)
    some(len(pairs))
    dcl[...] = dot(split(sg[...])[0], b, 1, 0) + dot(split(sg[...])[1], b, 1, 0)

    def use_level(k):
        @pl.when(bit(k) == 1)
        def _():
            level = f[k] if k == 0 else f[k] * off[k]
            lh, ll = split(level)
            y_acc[...] += coefx[k] * (dot(c, lh, 1, 0) + dot(c, ll, 1, 0))
            vh, vl = v_hi[k], v_lo[k]
            dcl[...] += dot(vh, lh, 1, 1) + dot(vh, ll, 1, 1) + dot(vl, lh, 1, 1)

    use_level(0)
    level_full(top)
    recv("F1C", f.at[1, pl.ds(half_other, half)], 0, bit(1) == 1)
    use_level(1)
    recv("CX", dt.at[pl.ds(pl.multiple_of(core * half + (1 - xbit) * quarter, quarter), quarter)], 1)
    send("CC", dt.at[own_rows], dt.at[own_rows], 0)
    for k in range(2, depth):
        recv(("FC", k), f.at[k, pl.ds(half_other, half)], 0, bit(k) == 1)
        use_level(k)
    y_out[...] = y_acc[...].astype(BF16)

    recv("R1A", g1.at[pl.ds(half_other, half)], 0, bit(1) == 0)
    recv("R0", r0, 0, bit(0) == 0)
    recv("CC", dt.at[pl.ds(half_other, half)], 0)
    cot = jnp.concatenate(
        [jnp.concatenate([cot_ref[2 * p], cot_ref[2 * p + 1]], axis=1) for p in range(heads // 2)], axis=1)
    ds_ = dt[...]
    ds_ = jnp.where(bit(1) == 1, ds_, up[1] * ds_ + g1[...])
    ds_ = jnp.where(bit(0) == 1, ds_, up[0] * ds_ + r0[...])
    ds_ = ds_ + after * cot
    dh, dl = split(ds_)
    uh, ul = u_hi[...], u_lo[...]
    sh, sl = split(sg[...])
    hx[mh, 0] = dcl[...]
    hx[mh, 1] = (dot(sh, c, 0, 0) + dot(sl, c, 0, 0)
                 + dot(uh, dh, 1, 1) + dot(uh, dl, 1, 1) + dot(ul, dh, 1, 1))

    def head_copy(j, slot):
        return pltpu.make_async_remote_copy(
            src_ref=hx.at[slot], dst_ref=hx.at[slot], send_sem=hs_sem.at[j], recv_sem=hr_sem.at[j],
            device_id={"heads": (mh + j) % nh}, device_id_type=MESH,
        )

    for j in range(1, nh):
        head_copy(j, mh).start()
    dx_out[...] = (dx_acc[...] + tsx[...] * (dot(b, dh, 1, 0) + dot(b, dl, 1, 0))).astype(BF16)
    for j in range(1, nh):
        head_copy(j, mh).wait_recv()
    dc, db = hx[0, 0], hx[0, 1]
    for v in range(1, nh):
        dc = dc + hx[v, 0]
        db = db + hx[v, 1]
    dc_out[...] = dc.astype(BF16)
    db_out[...] = db.astype(BF16)
    for j in range(1, nh):
        head_copy(j, mh).wait_send()
    for cp, when in pending:
        if when is None:
            cp.wait_send()
        else:
            pl.when(when)(cp.wait_send)
    pltpu.make_async_copy(gall.at[pl.ds(0, n - 1)], gall.at[pl.ds(0, n - 1)], gs_sem).wait()


def solution(mesh):
    n, nh = mesh.shape["seq"], mesh.shape["heads"]
    depth = n.bit_length() - 1

    def on_device(signal, b_in, c_in, step, decay_log, level_weight, skip, grad_out, state_cotangent):
        tokens, width = signal.shape
        heads = step.shape[0]
        rows = b_in.shape[1]
        half, quarter = rows // 2, rows // 4
        vm = lambda shape, dtype=F32: pltpu.VMEM(shape, dtype)
        count = 16 + 8 * depth
        spec = pl.BlockSpec(memory_space=pltpu.VMEM)
        return pl.pallas_call(
            functools.partial(kernel, n, depth, nh, heads, width, None),
            name="loglinear",
            out_shape=(
                jax.ShapeDtypeStruct((tokens, width), BF16),
                jax.ShapeDtypeStruct((tokens, width), BF16),
                jax.ShapeDtypeStruct((tokens, rows), BF16),
                jax.ShapeDtypeStruct((tokens, rows), BF16),
            ),
            in_specs=[spec] * 6 + [pl.BlockSpec(memory_space=pltpu.SMEM)] + [spec] * 2,
            out_specs=(spec,) * 4,
            scratch_shapes=[
                vm((n, 1, width)),
                vm((rows, width)),
                vm((half, width)),
                vm((depth, rows, width)),
                vm((depth, quarter, width)),
                vm((depth, rows, width)),
                vm((depth, half, width)),
                vm((depth, half, width)),
                vm((depth, quarter, width)),
                vm((rows, width)),
                vm((rows, width)),
                vm((depth, quarter, width)),
                vm((depth, quarter, width)),
                vm((rows, width)),
                vm((depth, tokens, width), BF16),
                vm((depth, tokens, width), BF16),
                vm((depth, tokens, width)),
                vm((tokens, width), BF16),
                vm((tokens, width), BF16),
                vm((tokens, width)),
                vm((tokens, width)),
                vm((tokens, width)),
                vm((tokens, tokens)),
                vm((tokens, rows)),
                vm((nh, 2, tokens, rows)),
                pltpu.SemaphoreType.DMA((count,)),
                pltpu.SemaphoreType.DMA((count,)),
                pltpu.SemaphoreType.DMA,
                pltpu.SemaphoreType.DMA,
                pltpu.SemaphoreType.DMA((nh,)),
                pltpu.SemaphoreType.DMA((nh,)),
            ],
            compiler_params=pltpu.CompilerParams(collective_id=0, has_side_effects=True),
        )(signal, b_in, c_in, step, decay_log, level_weight, skip, grad_out, state_cotangent)

    return jax.shard_map(
        on_device,
        mesh=mesh,
        in_specs=(
            P("seq", "heads"),
            P("seq", None),
            P("seq", None),
            P("heads", "seq"),
            P("heads", "seq"),
            P(None, "heads", "seq"),
            P("heads"),
            P("seq", "heads"),
            P("heads", None, None),
        ),
        out_specs=(P("seq", "heads"), P("seq", "heads"), P("seq", None), P("seq", None)),
        check_vma=False,
    )
```

time: 136 us -> 49.8 us (0.37)
  the two profiles are of different devices: /device:TPU:0 before, /device:TPU:3 now
where the time goes in v1:
time: 49.8 us; the launch traced here: 49.4 us
  Pallas kernels  41.5 us (83%)
  local copies, waits for them, and re-layouts  7.24 us (15%)
  between operations  0.65 us (1%)
    pallas_call x1, Pallas kernels, on_device(): pl.pallas_call(functools.partial(kernel, n, depth, nh, heads, width, None...  41.5 us
    unnamed x12, local copies, waits for them, and re-layouts  7.24 us

profile of v1, /device:TPU:3, one launch (start us, length us, event | category | flops | bytes accessed | tf_op | source)
XLA Modules:
  0.0 49.4 jit_solution(6290303888361961030)
XLA Ops:
  0.6 1.4 %copy.13.lw_ref = f32[8,10,128]{2,1,0:T(8,128)} copy(f32[8,10,128]{2,0,1:T(8,128)} %param.14) | data formatting | bytes 81920 | tf_op args[5]
  2.0 2.0 %copy.14.cot_ref = f32[10,128,64]{2,1,0:T(8,128)} copy(f32[10,128,64]{1,2,0:T(8,128)} %param.17) | data formatting | bytes 655360 | tf_op args[8]
  4.1 41.5 %loglinear.1 = (bf16[128,640]{1,0:T(8,128)(2,1)}, bf16[128,640]{1,0:T(8,128)(2,1)}, bf16[128,128]{1,0:T(8,128)(2,1)}, bf16[128,128]{1,0:T(8,128)(2,1)}) custom-call(bf16[128,640]{1,0:T(8,128)(2,1)} %x_ref.1, bf16[128,128]{1,0:T(8,128)(2,1)} %b_ref.1, bf16[128,128]{1,0:T(8,128)(2,1)} %c_ref.1, f32[10,128]{1,0:T(8,128)} %step_ref.1, f32[10,128]{1,0:T(8,128)} %decay_ref.1, ...), custom_call_target="tpu_custom_call" | custom-call | tf_op jit(solution)/shard_map/loglinear/pallas_call | solution.py:358
  45.6 0.0 copy-start
  45.6 1.6 %copy.19 = bf16[128,640]{1,0:T(8,128)(2,1)} copy(bf16[128,640]{1,0:T(8,128)(2,1)} %get-tuple-element.8) | data formatting | bytes 327680
  47.3 0.0 copy-done
  47.3 0.0 copy-start.2
  47.3 0.7 %copy.20 = bf16[128,640]{1,0:T(8,128)(2,1)} copy(bf16[128,640]{1,0:T(8,128)(2,1)S(1)} %copy-done) | data formatting | bytes 327680
  47.9 0.1 copy-done.2
  48.0 0.0 copy-start.1
  48.0 0.6 %copy.21 = bf16[128,128]{1,0:T(8,128)(2,1)} copy(bf16[128,128]{1,0:T(8,128)(2,1)S(1)} %copy-done.2) | data formatting | bytes 65536
  48.7 0.2 copy-done.1
  48.8 0.6 %copy.22 = bf16[128,128]{1,0:T(8,128)(2,1)} copy(bf16[128,128]{1,0:T(8,128)(2,1)S(1)} %copy-done.1) | data formatting | bytes 65536
Async XLA Ops:
  45.6 1.6 %copy-start = (bf16[128,640]{1,0:T(8,128)(2,1)S(1)}, bf16[128,640]{1,0:T(8,128)(2,1)}, u32[]{:S(2)}) copy-start(bf16[128,640]{1,0:T(8,128)(2,1)} %get-tuple-element.9) | copy-start | bytes 491524
  47.3 0.8 %copy-start.2 = (bf16[128,128]{1,0:T(8,128)(2,1)S(1)}, bf16[128,128]{1,0:T(8,128)(2,1)}, u32[]{:S(2)}) copy-start(bf16[128,128]{1,0:T(8,128)(2,1)} %get-tuple-element.10) | copy-start | bytes 98308
  48.0 0.8 %copy-start.1 = (bf16[128,128]{1,0:T(8,128)(2,1)S(1)}, bf16[128,128]{1,0:T(8,128)(2,1)}, u32[]{:S(2)}) copy-start(bf16[128,128]{1,0:T(8,128)(2,1)} %get-tuple-element.11) | copy-start | bytes 98308

commit v2 on v1

--- a/solution.py
+++ b/solution.py
@@ -23,12 +23,12 @@
 
 
 def kernel(
-    n, depth, nh, heads, width, has_rest,
+    n, depth, nh, heads, width,
     x_ref, b_ref, c_ref, step_ref, decay_ref, lw_ref, skip_ref, dy_ref, cot_ref,
     y_out, dx_out, db_out, dc_out,
-    gall, s_buf, t1, f, tq, g, rc, gh, rx, g1, r0, cs, cr, dt,
+    dself, dfar, s_buf, t1, f, tq, g, rc, gh, rx, g1, r0, cs, cr, dt,
     v_hi, v_lo, coefx, u_hi, u_lo, tsx, y_acc, dx_acc, sg, dcl, hx,
-    ssem, rsem, gs_sem, gr_sem, hs_sem, hr_sem,
+    ssem, rsem, hs_sem, hr_sem,
 ):
     me = lax.axis_index("seq")
     mh = lax.axis_index("heads")
@@ -50,11 +50,8 @@
 
     barrier = pltpu.get_barrier_semaphore()
 
-    def greet(j, carry):
-        pl.semaphore_signal(barrier, inc=1, device_id={"seq": (me + j) % n}, device_id_type=MESH)
-        return carry
-
-    lax.fori_loop(1, n, greet, 0)
+    for k in range(depth):
+        pl.semaphore_signal(barrier, inc=1, device_id={"seq": partner(k)}, device_id_type=MESH)
     for j in range(1, nh):
         pl.semaphore_signal(barrier, inc=1, device_id={"heads": (mh + j) % nh}, device_id_type=MESH)
 
@@ -107,24 +104,12 @@
     step = pad(step_ref[...])
     cum = jnp.dot(pad(decay_ref[...]), jnp.where(ti <= tj, 1.0, 0.0), precision=HIGH,
                   preferred_element_type=F32)
-    gall[me] = expand(cum)[tokens - 1:tokens, :]
+    dself[0] = expand(cum)[tokens - 1:tokens, :]
 
     x = x_ref[...]
     dy = dy_ref[...]
     b = b_ref[...]
     c = c_ref[...]
-
-    pl.semaphore_wait(barrier, n - 1 + nh - 1)
-
-    def share(j, carry):
-        pltpu.make_async_remote_copy(
-            src_ref=gall.at[me], dst_ref=gall.at[me], send_sem=gs_sem, recv_sem=gr_sem,
-            device_id={"seq": (me + j) % n}, device_id_type=MESH,
-        ).start()
-        return carry
-
-    lax.fori_loop(1, n, share, 0)
-
     tail = jnp.exp(cum[:, tokens - 1:tokens] - cum)
     ts = expand(tail * step)
     tsx[...] = ts
@@ -132,48 +117,92 @@
     u_hi[...] = uh
     u_lo[...] = ul
     s_buf[...] = dot(b, uh, 0, 0) + dot(b, ul, 0, 0)
+
+    pl.semaphore_wait(barrier, depth + nh - 1)
+    send(("D", 0), dself.at[0], dfar.at[0], 0)
     send("F0", s_buf, f.at[0], 0)
 
+    up = []
+    top = depth - 1
+    none = jnp.zeros((1, width), F32)
+
+    def retention_round(k):
+        recv(("D", k), dfar.at[k], k)
+        up.append(jnp.exp(jnp.where(bit(k) == 1, dself[k], dfar[k])))
+        if k < top:
+            dself[k + 1] = dself[k] + dfar[k]
+            send(("D", k + 1), dself.at[k + 1], dfar.at[k + 1], k + 1)
+
+    def before(first, last):
+        total = none
+        for j in range(first, last):
+            total = total + jnp.where(bit(j) == 1, dfar[j], 0.0)
+        return jnp.exp(total)
+
+    def merge(k, own, far):
+        is_up = bit(k) == 1
+        return jnp.where(is_up, own + up[k] * far, far + up[k] * own)
+
+    own_rows = pl.ds(half_own, half)
+    own_q = pl.ds(q_own, quarter)
+    side_q = pl.ds(pl.multiple_of(core * half + (1 - xbit) * quarter, quarter), quarter)
+    q_in_half = pl.ds(pl.multiple_of(xbit * quarter, quarter), quarter)
+    side_in_half = pl.ds(pl.multiple_of((1 - xbit) * quarter, quarter), quarter)
+
+    retention_round(0)
+    recv("F0", f.at[0], 0)
+    t1[...] = merge(0, s_buf[own_rows], f[0, own_rows])
+    send("F1A", t1.at[side_in_half], f.at[1, side_q], 1)
+
     ecum = jnp.exp(cum)
-    for k in range(depth):
+
+    def level_grad(k):
         @pl.when(bit(k) == 1)
         def _():
-            coef = expand(pad(lw_ref[k]) * ecum)
+            coef = expand(pad(lw_ref[:, k, :]) * ecum)
             coefx[k] = coef
             vh, vl = split(coef * dy.astype(F32))
             v_hi[k] = vh
             v_lo[k] = vl
             g[k] = dot(c, vh, 0, 0) + dot(c, vl, 0, 0)
-        if k == 0:
-            send("R0", g.at[0], r0, 0, bit(0) == 1)
-
-    everything = pltpu.make_async_copy(gall.at[pl.ds(0, n - 1)], gall.at[pl.ds(0, n - 1)], gr_sem)
-    everything.wait()
-    windows = lax.broadcasted_iota(jnp.int32, (n, 1, width), 0)
-    gv = gall[...]
-
-    def retention(mask):
-        return jnp.exp(jnp.sum(jnp.where(mask, gv, 0.0), axis=0))
-
-    up = [retention((windows >> k) == ((me >> k) | 1)) for k in range(depth)]
-    off = [None] + [retention(((windows >> k) == (me >> k)) & (windows < me)) for k in range(1, depth)]
-    after = retention(windows > me)
-
-    order = [1] + list(range(depth - 1, 1, -1))
+
+    order = list(range(top, 1, -1))
     for k in order:
+        level_grad(k)
+    retention_round(1)
+    inner = before(0, 2)
+
+    def scatter(k, scale):
         @pl.when(bit(k) == 1)
         def _():
-            g[k] = g[k] * off[k]
+            g[k] = g[k] * scale
         send(("RC", k), g.at[k, pl.ds(half_other, half)], rc.at[k], 0, bit(k) == 1)
 
-    def merge(k, own, far):
-        is_up = bit(k) == 1
-        return jnp.where(is_up, own + up[k] * far, far + up[k] * own)
-
-    recv("F0", f.at[0], 0)
-    own_rows = pl.ds(half_own, half)
-    t1[...] = merge(0, s_buf[own_rows], f[0, own_rows])
-    send("F1", t1, f.at[1, own_rows], 1)
+    for k in order:
+        scatter(k, inner)
+    level_grad(1)
+    scatter(1, before(0, 1))
+    level_grad(0)
+    send("R0", g.at[0], r0, 0, bit(0) == 1)
+
+    def fold_core(k):
+        recv(("RC", k), rc.at[k], 0, bit(k) == 1)
+
+        @pl.when(bit(k) == 1)
+        def _():
+            gh[k] = g[k, own_rows] + rc[k]
+
+    for k in order:
+        fold_core(k)
+        send(("RX", k), gh.at[k, side_in_half], rx.at[k], 1, bit(k) == 1)
+    for k in range(2, top):
+        retention_round(k)
+    recv("F1A", f.at[1, own_q], 1)
+    tq[2] = merge(1, t1[q_in_half], f[1, own_q])
+    send(("F", 2), tq.at[2], f.at[2, own_q], 2, bit(2) == 0 if top == 2 else None)
+    fold_core(1)
+    send("R1X", gh.at[1], g1.at[own_rows], 1, bit(1) == 1)
+    send("F1B", t1.at[q_in_half], f.at[1, own_q], 1, bit(1) == 0)
 
     scores = dot(c, b, 1, 1)
     cum_t = cum.T
@@ -215,47 +244,18 @@
             if pairs:
                 pair(pairs.pop(0))
 
-    some(1)
-    for k in order:
-        recv(("RC", k), rc.at[k], 0, bit(k) == 1)
-
-        @pl.when(bit(k) == 1)
-        def _():
-            gh[k] = g[k, own_rows] + rc[k]
-        if k >= 2:
-            send(("RX", k), gh.at[k, pl.ds(pl.multiple_of((1 - xbit) * quarter, quarter), quarter)],
-                 rx.at[k], 1, bit(k) == 1)
-        else:
-            send("R1X", gh.at[1], g1.at[own_rows], 1, bit(1) == 1)
-
-    own_q = pl.ds(q_own, quarter)
-    q_in_half = pl.ds(pl.multiple_of(xbit * quarter, quarter), quarter)
-    recv("F1", f.at[1, own_rows], 1)
-    tq[2] = merge(1, t1[q_in_half], f[1, own_q])
-    top = depth - 1
-    send(("F", 2), tq.at[2], f.at[2, own_q], 2, bit(2) == 0 if top == 2 else None)
-    send("F1C", f.at[1, own_rows], f.at[1, own_rows], 0, bit(1) == 1)
-    some(1)
-
-    recv("R1X", g1.at[own_rows], 1, bit(1) == 0)
-    send("R1A", g1.at[own_rows], g1.at[own_rows], 0, bit(1) == 0)
-    cs[0] = jnp.zeros((quarter, width), F32)
-    carry_slot = cs.at[0]
-
-    def slab_grad(k):
-        recv(("RX", k), rx.at[k], 1, bit(k) == 1)
+    some(2)
 
     def level_full(k):
-        recv(("FX", k), f.at[k, pl.ds(pl.multiple_of(core * half + (1 - xbit) * quarter, quarter), quarter)], 1,
-             bit(k) == 1)
+        recv(("FX", k), f.at[k, side_q], 1, bit(k) == 1)
         send(("FC", k), f.at[k, own_rows], f.at[k, own_rows], 0, bit(k) == 1)
 
     carry = None
     for r in range(2, depth):
         kb = top - (r - 2)
-        slab_grad(kb)
+        recv(("RX", kb), rx.at[kb], 1, bit(kb) == 1)
         is_up = bit(kb) == 1
-        grad = jnp.where(is_up, gh[kb, q_in_half] + rx[kb], 0.0)
+        grad = jnp.where(is_up, before(2, kb) * (gh[kb, q_in_half] + rx[kb]), 0.0)
         if carry is None:
             cs[kb] = grad
             send(("C", kb), cs.at[kb], cr.at[kb], kb, is_up)
@@ -275,15 +275,28 @@
             carry = jnp.where(is_up, 0.0, cr[kb])
         else:
             carry = jnp.where(is_up, carry, up[kb] * carry) + cr[kb]
-    dt[own_q] = carry
-    send("CX", dt.at[own_q], dt.at[own_q], 1)
+    has_carry = (me // 4) != (n // 4 - 1)
+
+    @pl.when(has_carry)
+    def _():
+        dt[own_q] = carry
+
+    @pl.when(jnp.logical_not(has_carry))
+    def _():
+        dt[...] = jnp.zeros_like(dt)
+
+    send("CX", dt.at[own_q], dt.at[own_q], 1, has_carry)
+    recv("F1B", f.at[1, side_q], 1, bit(1) == 1)
+    send("F1C", f.at[1, own_rows], f.at[1, own_rows], 0, bit(1) == 1)
+    recv("R1X", g1.at[own_rows], 1, bit(1) == 0)
+    send("R1A", g1.at[own_rows], g1.at[own_rows], 0, bit(1) == 0)
     some(len(pairs))
     dcl[...] = dot(split(sg[...])[0], b, 1, 0) + dot(split(sg[...])[1], b, 1, 0)
 
     def use_level(k):
         @pl.when(bit(k) == 1)
         def _():
-            level = f[k] if k == 0 else f[k] * off[k]
+            level = f[k] if k == 0 else f[k] * before(0, k)
             lh, ll = split(level)
             y_acc[...] += coefx[k] * (dot(c, lh, 1, 0) + dot(c, ll, 1, 0))
             vh, vl = v_hi[k], v_lo[k]
@@ -293,40 +306,49 @@
     level_full(top)
     recv("F1C", f.at[1, pl.ds(half_other, half)], 0, bit(1) == 1)
     use_level(1)
-    recv("CX", dt.at[pl.ds(pl.multiple_of(core * half + (1 - xbit) * quarter, quarter), quarter)], 1)
-    send("CC", dt.at[own_rows], dt.at[own_rows], 0)
+    recv("CX", dt.at[side_q], 1, has_carry)
+    send("CC", dt.at[own_rows], dt.at[own_rows], 0, has_carry)
     for k in range(2, depth):
         recv(("FC", k), f.at[k, pl.ds(half_other, half)], 0, bit(k) == 1)
         use_level(k)
+
+    def head_copy(j, part):
+        return pltpu.make_async_remote_copy(
+            src_ref=hx.at[mh, part], dst_ref=hx.at[mh, part],
+            send_sem=hs_sem.at[j, part], recv_sem=hr_sem.at[j, part],
+            device_id={"heads": (mh + j) % nh}, device_id_type=MESH,
+        )
+
+    hx[mh, 0] = dcl[...]
+    for j in range(1, nh):
+        head_copy(j, 0).start()
     y_out[...] = y_acc[...].astype(BF16)
 
     recv("R1A", g1.at[pl.ds(half_other, half)], 0, bit(1) == 0)
     recv("R0", r0, 0, bit(0) == 0)
-    recv("CC", dt.at[pl.ds(half_other, half)], 0)
+    recv("CC", dt.at[pl.ds(half_other, half)], 0, has_carry)
+    retention_round(top)
     cot = jnp.concatenate(
-        [jnp.concatenate([cot_ref[2 * p], cot_ref[2 * p + 1]], axis=1) for p in range(heads // 2)], axis=1)
+        [jnp.concatenate([cot_ref[2 * p], cot_ref[2 * p + 1]], axis=0).T for p in range(heads // 2)], axis=1)
     ds_ = dt[...]
     ds_ = jnp.where(bit(1) == 1, ds_, up[1] * ds_ + g1[...])
     ds_ = jnp.where(bit(0) == 1, ds_, up[0] * ds_ + r0[...])
-    ds_ = ds_ + after * cot
+    later = none
+    for j in range(depth):
+        later = later + jnp.where(bit(j) == 0, dfar[j], 0.0)
+    ds_ = ds_ + jnp.exp(later) * cot
     dh, dl = split(ds_)
     uh, ul = u_hi[...], u_lo[...]
     sh, sl = split(sg[...])
-    hx[mh, 0] = dcl[...]
     hx[mh, 1] = (dot(sh, c, 0, 0) + dot(sl, c, 0, 0)
                  + dot(uh, dh, 1, 1) + dot(uh, dl, 1, 1) + dot(ul, dh, 1, 1))
 
-    def head_copy(j, slot):
-        return pltpu.make_async_remote_copy(
-            src_ref=hx.at[slot], dst_ref=hx.at[slot], send_sem=hs_sem.at[j], recv_sem=hr_sem.at[j],
-            device_id={"heads": (mh + j) % nh}, device_id_type=MESH,
-        )
-
     for j in range(1, nh):
-        head_copy(j, mh).start()
+        head_copy(j, 1).start()
     dx_out[...] = (dx_acc[...] + tsx[...] * (dot(b, dh, 1, 0) + dot(b, dl, 1, 0))).astype(BF16)
     for j in range(1, nh):
-        head_copy(j, mh).wait_recv()
+        head_copy(j, 0).wait_recv()
+        head_copy(j, 1).wait_recv()
     dc, db = hx[0, 0], hx[0, 1]
     for v in range(1, nh):
         dc = dc + hx[v, 0]
@@ -334,13 +356,18 @@
     dc_out[...] = dc.astype(BF16)
     db_out[...] = db.astype(BF16)
     for j in range(1, nh):
-        head_copy(j, mh).wait_send()
+        head_copy(j, 0).wait_send()
+        head_copy(j, 1).wait_send()
     for cp, when in pending:
         if when is None:
             cp.wait_send()
         else:
             pl.when(when)(cp.wait_send)
-    pltpu.make_async_copy(gall.at[pl.ds(0, n - 1)], gall.at[pl.ds(0, n - 1)], gs_sem).wait()
+
+
+def hand_over(*refs):
+    for src, dst in zip(refs[:4], refs[4:]):
+        dst[...] = src[...]
 
 
 def solution(mesh):
@@ -355,8 +382,8 @@
         vm = lambda shape, dtype=F32: pltpu.VMEM(shape, dtype)
         count = 16 + 8 * depth
         spec = pl.BlockSpec(memory_space=pltpu.VMEM)
-        return pl.pallas_call(
-            functools.partial(kernel, n, depth, nh, heads, width, None),
+        results = pl.pallas_call(
+            functools.partial(kernel, n, depth, nh, heads, width),
             name="loglinear",
             out_shape=(
                 jax.ShapeDtypeStruct((tokens, width), BF16),
@@ -367,7 +394,8 @@
             in_specs=[spec] * 6 + [pl.BlockSpec(memory_space=pltpu.SMEM)] + [spec] * 2,
             out_specs=(spec,) * 4,
             scratch_shapes=[
-                vm((n, 1, width)),
+                vm((depth, 1, width)),
+                vm((depth, 1, width)),
                 vm((rows, width)),
                 vm((half, width)),
                 vm((depth, rows, width)),
@@ -394,13 +422,19 @@
                 vm((nh, 2, tokens, rows)),
                 pltpu.SemaphoreType.DMA((count,)),
                 pltpu.SemaphoreType.DMA((count,)),
-                pltpu.SemaphoreType.DMA,
-                pltpu.SemaphoreType.DMA,
-                pltpu.SemaphoreType.DMA((nh,)),
-                pltpu.SemaphoreType.DMA((nh,)),
+                pltpu.SemaphoreType.DMA((nh, 2)),
+                pltpu.SemaphoreType.DMA((nh, 2)),
             ],
             compiler_params=pltpu.CompilerParams(collective_id=0, has_side_effects=True),
-        )(signal, b_in, c_in, step, decay_log, level_weight, skip, grad_out, state_cotangent)
+        )(signal, b_in, c_in, step, decay_log, level_weight.transpose(1, 0, 2), skip, grad_out,
+          state_cotangent.transpose(0, 2, 1))
+        return pl.pallas_call(
+            hand_over,
+            name="handover",
+            out_shape=tuple(jax.ShapeDtypeStruct(r.shape, r.dtype) for r in results),
+            in_specs=[spec] * 4,
+            out_specs=(spec,) * 4,
+        )(*results)
 
     return jax.shard_map(
         on_device,

time: 49.8 us -> 34.8 us (0.70)
  the two profiles are of different devices: /device:TPU:3 before, /device:TPU:0 now
where the time goes in v2:
time: 34.8 us; the launch traced here: 34.2 us
  Pallas kernels  33.6 us (97%)
  between operations  0.64 us (2%)
    pallas_call x1, Pallas kernels, on_device(): pl.pallas_call(functools.partial(kernel, n, depth, nh, heads, width), nam...  31.8 us
    pallas_call x1, Pallas kernels, on_device(): pl.pallas_call(hand_over, name='handover', out_shape=tuple((jax.ShapeDtyp...  1.75 us

profile of v2, /device:TPU:0, one launch (start us, length us, event | category | flops | bytes accessed | tf_op | source)
XLA Modules:
  0.0 34.2 jit_solution(66846889991585335)
XLA Ops:
  0.6 31.8 %loglinear.1 = (bf16[128,640]{1,0:T(8,128)(2,1)}, bf16[128,640]{1,0:T(8,128)(2,1)}, bf16[128,128]{1,0:T(8,128)(2,1)}, bf16[128,128]{1,0:T(8,128)(2,1)}) custom-call(bf16[128,640]{1,0:T(8,128)(2,1)} %x_ref.1, bf16[128,128]{1,0:T(8,128)(2,1)} %b_ref.1, bf16[128,128]{1,0:T(8,128)(2,1)} %c_ref.1, f32[10,128]{1,0:T(8,128)} %step_ref.1, f32[10,128]{1,0:T(8,128)} %decay_ref.1, ...), custom_call_target="tpu_custom_call" | custom-call | tf_op jit(solution)/shard_map/loglinear/pallas_call | solution.py:385
  32.5 1.8 %handover.1 = (bf16[128,640]{1,0:T(8,128)(2,1)}, bf16[128,640]{1,0:T(8,128)(2,1)}, bf16[128,128]{1,0:T(8,128)(2,1)}, bf16[128,128]{1,0:T(8,128)(2,1)}) custom-call(bf16[128,640]{1,0:T(8,128)(2,1)} %get-tuple-element.8.refs_0_, bf16[128,640]{1,0:T(8,128)(2,1)} %get-tuple-element.9.refs_1_, bf16[128,128]{1,0:T(8,128)(2,1)} %get-tuple-element.10.refs_2_, ...), custom_call_target="tpu_custom_call" | custom-call | tf_op jit(solution)/shard_map/handover/pallas_call | solution.py:431

commit v3 on v2

--- a/solution.py
+++ b/solution.py
@@ -11,6 +11,7 @@
 HIGH = lax.Precision.HIGHEST
 F32 = jnp.float32
 BF16 = jnp.bfloat16
+CHUNKS = 2
 
 
 def split(v):
@@ -110,51 +111,9 @@
     dy = dy_ref[...]
     b = b_ref[...]
     c = c_ref[...]
-    tail = jnp.exp(cum[:, tokens - 1:tokens] - cum)
-    ts = expand(tail * step)
-    tsx[...] = ts
-    uh, ul = split(ts * x.astype(F32))
-    u_hi[...] = uh
-    u_lo[...] = ul
-    s_buf[...] = dot(b, uh, 0, 0) + dot(b, ul, 0, 0)
-
-    pl.semaphore_wait(barrier, depth + nh - 1)
-    send(("D", 0), dself.at[0], dfar.at[0], 0)
-    send("F0", s_buf, f.at[0], 0)
-
-    up = []
+    ecum = jnp.exp(cum)
     top = depth - 1
-    none = jnp.zeros((1, width), F32)
-
-    def retention_round(k):
-        recv(("D", k), dfar.at[k], k)
-        up.append(jnp.exp(jnp.where(bit(k) == 1, dself[k], dfar[k])))
-        if k < top:
-            dself[k + 1] = dself[k] + dfar[k]
-            send(("D", k + 1), dself.at[k + 1], dfar.at[k + 1], k + 1)
-
-    def before(first, last):
-        total = none
-        for j in range(first, last):
-            total = total + jnp.where(bit(j) == 1, dfar[j], 0.0)
-        return jnp.exp(total)
-
-    def merge(k, own, far):
-        is_up = bit(k) == 1
-        return jnp.where(is_up, own + up[k] * far, far + up[k] * own)
-
-    own_rows = pl.ds(half_own, half)
-    own_q = pl.ds(q_own, quarter)
-    side_q = pl.ds(pl.multiple_of(core * half + (1 - xbit) * quarter, quarter), quarter)
-    q_in_half = pl.ds(pl.multiple_of(xbit * quarter, quarter), quarter)
-    side_in_half = pl.ds(pl.multiple_of((1 - xbit) * quarter, quarter), quarter)
-
-    retention_round(0)
-    recv("F0", f.at[0], 0)
-    t1[...] = merge(0, s_buf[own_rows], f[0, own_rows])
-    send("F1A", t1.at[side_in_half], f.at[1, side_q], 1)
-
-    ecum = jnp.exp(cum)
+    order = list(range(top, 1, -1))
 
     def level_grad(k):
         @pl.when(bit(k) == 1)
@@ -166,43 +125,91 @@
             v_lo[k] = vl
             g[k] = dot(c, vh, 0, 0) + dot(c, vl, 0, 0)
 
-    order = list(range(top, 1, -1))
     for k in order:
         level_grad(k)
-    retention_round(1)
-    inner = before(0, 2)
-
-    def scatter(k, scale):
+    tail = jnp.exp(cum[:, tokens - 1:tokens] - cum)
+    ts = expand(tail * step)
+    tsx[...] = ts
+    uh, ul = split(ts * x.astype(F32))
+    u_hi[...] = uh
+    u_lo[...] = ul
+    s_buf[...] = dot(b, uh, 0, 0) + dot(b, ul, 0, 0)
+
+    pl.semaphore_wait(barrier, depth + nh - 1)
+    send(("D", 0), dself.at[0], dfar.at[0], 0)
+    send(("RC", top), g.at[top, pl.ds(half_other, half)], rc.at[top], 0, bit(top) == 1)
+    send("F0", s_buf, f.at[0], 0)
+    for k in order[1:] + [1]:
+        if k == 1:
+            level_grad(1)
+        send(("RC", k), g.at[k, pl.ds(half_other, half)], rc.at[k], 0, bit(k) == 1)
+    level_grad(0)
+    send("R0", g.at[0], r0, 0, bit(0) == 1)
+
+    up = []
+    down = []
+    none = jnp.zeros((1, width), F32)
+
+    def retention_round(k):
+        recv(("D", k), dfar.at[k], k)
+        up.append(jnp.exp(jnp.where(bit(k) == 1, dself[k], dfar[k])))
+        down.append(jnp.exp(jnp.where(bit(k) == 1, dfar[k], dself[k])))
+        if k < top:
+            dself[k + 1] = dself[k] + dfar[k]
+            send(("D", k + 1), dself.at[k + 1], dfar.at[k + 1], k + 1)
+
+    def before(first, last):
+        total = none
+        for j in range(first, last):
+            total = total + jnp.where(bit(j) == 1, dfar[j], 0.0)
+        return jnp.exp(total)
+
+    def merge(k, own, far):
+        is_up = bit(k) == 1
+        return jnp.where(is_up, own + up[k] * far, far + up[k] * own)
+
+    def unmerge(k, own, far):
+        is_up = bit(k) == 1
+        return jnp.where(is_up, own * down[k] + far, own + far * down[k])
+
+    sub = quarter // CHUNKS
+    chunks = range(CHUNKS)
+
+    def piece(start, m):
+        return pl.ds(pl.multiple_of(start + m * sub, sub), sub)
+
+    own_in, side_in = xbit * quarter, (1 - xbit) * quarter
+    own_start, side_start = core * half + own_in, core * half + side_in
+    own_rows = pl.ds(half_own, half)
+    own_q = pl.ds(q_own, quarter)
+    side_q = pl.ds(pl.multiple_of(core * half + (1 - xbit) * quarter, quarter), quarter)
+    q_in_half = pl.ds(pl.multiple_of(xbit * quarter, quarter), quarter)
+
+    retention_round(0)
+
+    def fold_core(k):
+        recv(("RC", k), rc.at[k], 0, bit(k) == 1)
+
         @pl.when(bit(k) == 1)
         def _():
-            g[k] = g[k] * scale
-        send(("RC", k), g.at[k, pl.ds(half_other, half)], rc.at[k], 0, bit(k) == 1)
-
-    for k in order:
-        scatter(k, inner)
-    level_grad(1)
-    scatter(1, before(0, 1))
-    level_grad(0)
-    send("R0", g.at[0], r0, 0, bit(0) == 1)
-
-    def fold_core(k):
-        recv(("RC", k), rc.at[k], 0, bit(k) == 1)
-
-        @pl.when(bit(k) == 1)
-        def _():
-            gh[k] = g[k, own_rows] + rc[k]
-
-    for k in order:
+            gh[k] = unmerge(0, g[k, own_rows], rc[k])
+
+    def send_side(k):
+        for m in chunks:
+            send(("RX", k, m), gh.at[k, piece(side_in, m)], rx.at[k, pl.ds(m * sub, sub)], 1, bit(k) == 1)
+
+    fold_core(top)
+    send_side(top)
+    recv("F0", f.at[0], 0)
+    t1[...] = merge(0, s_buf[own_rows], f[0, own_rows])
+    for m in chunks:
+        send(("F1A", m), t1.at[piece(side_in, m)], f.at[1, piece(side_start, m)], 1)
+    for k in order[1:]:
         fold_core(k)
-        send(("RX", k), gh.at[k, side_in_half], rx.at[k], 1, bit(k) == 1)
+        send_side(k)
+    retention_round(1)
     for k in range(2, top):
         retention_round(k)
-    recv("F1A", f.at[1, own_q], 1)
-    tq[2] = merge(1, t1[q_in_half], f[1, own_q])
-    send(("F", 2), tq.at[2], f.at[2, own_q], 2, bit(2) == 0 if top == 2 else None)
-    fold_core(1)
-    send("R1X", gh.at[1], g1.at[own_rows], 1, bit(1) == 1)
-    send("F1B", t1.at[q_in_half], f.at[1, own_q], 1, bit(1) == 0)
 
     scores = dot(c, b, 1, 1)
     cum_t = cum.T
@@ -244,48 +251,86 @@
             if pairs:
                 pair(pairs.pop(0))
 
-    some(2)
-
-    def level_full(k):
-        recv(("FX", k), f.at[k, side_q], 1, bit(k) == 1)
-        send(("FC", k), f.at[k, own_rows], f.at[k, own_rows], 0, bit(k) == 1)
-
-    carry = None
-    for r in range(2, depth):
-        kb = top - (r - 2)
-        recv(("RX", kb), rx.at[kb], 1, bit(kb) == 1)
-        is_up = bit(kb) == 1
-        grad = jnp.where(is_up, before(2, kb) * (gh[kb, q_in_half] + rx[kb]), 0.0)
-        if carry is None:
-            cs[kb] = grad
-            send(("C", kb), cs.at[kb], cr.at[kb], kb, is_up)
+    some(1)
+
+    def send_level(k, m, own, far):
+        tq[k, pl.ds(m * sub, sub)] = merge(k - 1, own, far)
+        send(("F", k, m), tq.at[k, pl.ds(m * sub, sub)], f.at[k, piece(own_start, m)], k,
+             bit(k) == 0 if k == top else None)
+
+    carry = [None] * CHUNKS
+
+    def start_carry(k, m):
+        rows_m = pl.ds(m * sub, sub)
+        recv(("RX", k, m), rx.at[k, rows_m], 1, bit(k) == 1)
+        is_up = bit(k) == 1
+        grad = jnp.where(is_up, before(2, k) * unmerge(1, gh[k, piece(own_in, m)], rx[k, rows_m]), 0.0)
+        if k == top:
+            cs[k, rows_m] = grad
         else:
-            cs[kb] = jnp.where(is_up, up[kb] * carry + grad, carry)
-            send(("C", kb), cs.at[kb], cr.at[kb], kb)
-        some(1)
-        recv(("F", r), f.at[r, own_q], r, bit(r) == 1 if r == top else None)
-        if r < top:
-            tq[r + 1] = merge(r, tq[r], f[r, own_q])
-            send(("F", r + 1), tq.at[r + 1], f.at[r + 1, own_q], r + 1, bit(r + 1) == 0 if r + 1 == top else None)
-        send(("FX", r), f.at[r, own_q], f.at[r, own_q], 1, bit(r) == 1)
-        if r > 2:
-            level_full(r - 1)
-        recv(("C", kb), cr.at[kb], kb, bit(kb) == 0 if kb == top else None)
-        if carry is None:
-            carry = jnp.where(is_up, 0.0, cr[kb])
+            cs[k, rows_m] = jnp.where(is_up, up[k] * carry[m] + grad, carry[m])
+        send(("C", k, m), cs.at[k, rows_m], cr.at[k, rows_m], k, is_up if k == top else None)
+
+    def end_carry(k, m):
+        rows_m = pl.ds(m * sub, sub)
+        recv(("C", k, m), cr.at[k, rows_m], k, bit(k) == 0 if k == top else None)
+        is_up = bit(k) == 1
+        if k == top:
+            carry[m] = jnp.where(is_up, 0.0, cr[k, rows_m])
         else:
-            carry = jnp.where(is_up, carry, up[kb] * carry) + cr[kb]
+            carry[m] = jnp.where(is_up, carry[m], up[k] * carry[m]) + cr[k, rows_m]
+
+    for m in chunks:
+        start_carry(top, m)
+    for m in chunks:
+        recv(("F1A", m), f.at[1, piece(own_start, m)], 1)
+        send_level(2, m, t1[piece(own_in, m)], f[1, piece(own_start, m)])
+    fold_core(1)
+    send("R1X", gh.at[1], g1.at[own_rows], 1, bit(1) == 1)
+    send("F1B", t1.at[q_in_half], f.at[1, own_q], 1, bit(1) == 0)
     has_carry = (me // 4) != (n // 4 - 1)
-
-    @pl.when(has_carry)
-    def _():
-        dt[own_q] = carry
 
     @pl.when(jnp.logical_not(has_carry))
     def _():
         dt[...] = jnp.zeros_like(dt)
 
-    send("CX", dt.at[own_q], dt.at[own_q], 1, has_carry)
+    def level_full(k):
+        for m in chunks:
+            recv(("FX", k, m), f.at[k, piece(side_start, m)], 1, bit(k) == 1)
+        send(("FC", k), f.at[k, own_rows], f.at[k, own_rows], 0, bit(k) == 1)
+
+    def forward_round(r):
+        for m in chunks:
+            here = f.at[r, piece(own_start, m)]
+            recv(("F", r, m), here, r, bit(r) == 1 if r == top else None)
+            if r < top:
+                send_level(r + 1, m, tq[r, pl.ds(m * sub, sub)], f[r, piece(own_start, m)])
+            send(("FX", r, m), here, here, 1, bit(r) == 1)
+        if r > 2:
+            level_full(r - 1)
+
+    def store_carry(m):
+        @pl.when(has_carry)
+        def _():
+            dt[piece(own_start, m)] = carry[m]
+        send(("CX", m), dt.at[piece(own_start, m)], dt.at[piece(own_start, m)], 1, has_carry)
+
+    def backward_round(k):
+        for m in chunks:
+            end_carry(k, m)
+            if k > 2:
+                start_carry(k - 1, m)
+            else:
+                store_carry(m)
+
+    for r in range(2, depth):
+        some(1)
+        if r < top:
+            forward_round(r)
+            backward_round(top + 2 - r)
+        else:
+            backward_round(top + 2 - r)
+            forward_round(r)
     recv("F1B", f.at[1, side_q], 1, bit(1) == 1)
     send("F1C", f.at[1, own_rows], f.at[1, own_rows], 0, bit(1) == 1)
     recv("R1X", g1.at[own_rows], 1, bit(1) == 0)
@@ -306,7 +351,8 @@
     level_full(top)
     recv("F1C", f.at[1, pl.ds(half_other, half)], 0, bit(1) == 1)
     use_level(1)
-    recv("CX", dt.at[side_q], 1, has_carry)
+    for m in chunks:
+        recv(("CX", m), dt.at[piece(side_start, m)], 1, has_carry)
     send("CC", dt.at[own_rows], dt.at[own_rows], 0, has_carry)
     for k in range(2, depth):
         recv(("FC", k), f.at[k, pl.ds(half_other, half)], 0, bit(k) == 1)
@@ -380,7 +426,7 @@
         rows = b_in.shape[1]
         half, quarter = rows // 2, rows // 4
         vm = lambda shape, dtype=F32: pltpu.VMEM(shape, dtype)
-        count = 16 + 8 * depth
+        count = 16 + 4 * CHUNKS + (4 + 4 * CHUNKS) * depth
         spec = pl.BlockSpec(memory_space=pltpu.VMEM)
         results = pl.pallas_call(
             functools.partial(kernel, n, depth, nh, heads, width),

time: 34.8 us -> 32.8 us (0.943)
  the two profiles are of different devices: /device:TPU:0 before, /device:TPU:27 now
where the time goes in v3:
time: 32.8 us; the launch traced here: 32.7 us
  Pallas kernels  32 us (98%)
  between operations  0.64 us (2%)
    pallas_call x1, Pallas kernels, on_device(): pl.pallas_call(functools.partial(kernel, n, depth, nh, heads, width), nam...  30.3 us
    pallas_call x1, Pallas kernels, on_device(): pl.pallas_call(hand_over, name='handover', out_shape=tuple((jax.ShapeDtyp...  1.75 us

profile of v3, /device:TPU:27, one launch (start us, length us, event | category | flops | bytes accessed | tf_op | source)
XLA Modules:
  0.0 32.7 jit_solution(8294923533874264924)
XLA Ops:
  0.6 30.3 %loglinear.1 = (bf16[128,640]{1,0:T(8,128)(2,1)}, bf16[128,640]{1,0:T(8,128)(2,1)}, bf16[128,128]{1,0:T(8,128)(2,1)}, bf16[128,128]{1,0:T(8,128)(2,1)}) custom-call(bf16[128,640]{1,0:T(8,128)(2,1)} %x_ref.1, bf16[128,128]{1,0:T(8,128)(2,1)} %b_ref.1, bf16[128,128]{1,0:T(8,128)(2,1)} %c_ref.1, f32[10,128]{1,0:T(8,128)} %step_ref.1, f32[10,128]{1,0:T(8,128)} %decay_ref.1, ...), custom_call_target="tpu_custom_call" | custom-call | tf_op jit(solution)/shard_map/loglinear/pallas_call | solution.py:431
  30.9 1.8 %handover.1 = (bf16[128,640]{1,0:T(8,128)(2,1)}, bf16[128,640]{1,0:T(8,128)(2,1)}, bf16[128,128]{1,0:T(8,128)(2,1)}, bf16[128,128]{1,0:T(8,128)(2,1)}) custom-call(bf16[128,640]{1,0:T(8,128)(2,1)} %get-tuple-element.8.refs_0_, bf16[128,640]{1,0:T(8,128)(2,1)} %get-tuple-element.9.refs_1_, bf16[128,128]{1,0:T(8,128)(2,1)} %get-tuple-element.10.refs_2_, ...), custom_call_target="tpu_custom_call" | custom-call | tf_op jit(solution)/shard_map/handover/pallas_call | solution.py:477
